TPU v7x, 128 devices: a whole 4x4x4 slice. The times are simulated.
128 devices in a mesh: leaf: 128 (over y, z, x, core).
Axes of the slice: x: 4, y: 4, z: 4, core: 2. Of those that a mesh axis runs over, the one named last changes fastest.
Arguments:
- right_hand: float32 [2048, 32, 256], P('leaf')
- leaf_live: int32 [2048], P('leaf'), may hold values from 0 to 1, as said below
- near_index: int32 [2048, 6], P('leaf'), may hold values from 0 to 2047, as said below
- near_tile: bfloat16 [2048, 6, 256, 256], P('leaf'), may hold values from -1 to 5
- far_index: int32 [2048, 8], P('leaf'), may hold values from 0 to 2047, as said below
- far_couple: bfloat16 [2048, 8, 64, 64], P('leaf'), may hold values from -0.25 to 0.25
- leaf_basis: bfloat16 [2048, 64, 256], P('leaf'), may hold values from -0.375 to 0.375
- leaf_transfer: bfloat16 [2048, 64, 64], P('leaf'), may hold values from -0.1875 to 0.1875
- tree_up: bfloat16 [254, 64, 64], replicated, may hold values from -0.5 to 0.5
- tree_couple: bfloat16 [254, 64, 64], replicated, may hold values from -0.75 to 0.75
Outputs:
- basis_next: float32 [2048, 32, 256], P('leaf')
- hessenberg: float32 [6, 32], replicated
Inputs may be any that keep to these rules, and one draw needn't show every extreme that they name: `leaf_live`: each device's 16 slots hold between 5 and 16 live leaves, both counts reached on some device; which slots are live is arbitrary. `near_index`: entry 0 of each row is the row's own slot; every entry lies within 2 slots of its row's slot, and some entry lies exactly 2 away; entries may name dead slots. `far_index`: every entry lies within 16 slots of its row's slot, and some entry lies exactly 16 away; entries may name dead slots.
All inputs are finite; a program needn't handle non-finite values.
Results may differ from a plain program's by a relative error of at most 0.009.
Values may be sent and summed in bfloat16 or wider, within the bound.
No kernel may reach another device: no remote copies, remote signals or barrier semaphores. Data moves between devices by JAX's collectives and lax.ppermute only.
A program may use at most 128 MiB of HBM per device.

v0:
```python
import jax
import jax.numpy as jnp
from jax import lax
from jax.sharding import PartitionSpec as P

epsilon = 1e-06


def with_halo(array, sides, width):
    for axis, dim in sides:
        size, length = (lax.axis_size(axis), array.shape[dim])
        up = [(i, (i + 1) % size) for i in range(size - 1)]
        down = [(j, i) for i, j in up]
        last = lax.slice_in_dim(array, length - width, length, axis=dim)
        initial = lax.slice_in_dim(array, 0, width, axis=dim)
        before = lax.ppermute(last, axis, up)
        after = lax.ppermute(initial, axis, down)
        array = jnp.concatenate([before, array, after], axis=dim)
    return array


def swapped(array, axis, stride):
    return lax.ppermute(array, axis, [(i, i ^ 1 << stride) for i in range(lax.axis_size(axis))])


def apply_operator(
    vector,
    leaf_live,
    near_index,
    near_tile,
    far_index,
    far_couple,
    leaf_basis,
    leaf_transfer,
    tree_up,
    tree_couple,
):
    position = lax.axis_index("leaf")
    device_total = lax.axis_size("leaf")
    slot_count = vector.shape[0]
    live_mask = leaf_live.astype(jnp.float32)[:, None, None]
    inputs = (vector * live_mask).astype(jnp.bfloat16)
    padded = with_halo(inputs, (("leaf", 0),), slot_count)
    local_near = near_index - (position * slot_count - slot_count)
    columns = padded[local_near]
    near = jnp.einsum("inrp,inpq->irq", columns, near_tile, preferred_element_type=jnp.float32)
    moments = jnp.einsum(
        "irp,ikp->irk", inputs, leaf_basis, preferred_element_type=jnp.float32
    ).astype(jnp.bfloat16)
    moment_pad = with_halo(moments, (("leaf", 0),), slot_count)
    local_far = far_index - (position * slot_count - slot_count)
    far_term = jnp.einsum(
        "ifrk,ifkj->irj", moment_pad[local_far], far_couple, preferred_element_type=jnp.float32
    )
    box_moment = jnp.einsum(
        "irk,ikj->rj", moments, leaf_transfer, preferred_element_type=jnp.float32
    ).astype(jnp.bfloat16)
    levels = device_total.bit_length() - 1
    locals_list = []
    current = box_moment
    for level in range(levels):
        level_first = 2 * device_total - 2 * (device_total >> level)
        own_node = level_first + (position >> level)
        other_node = level_first + (position >> level ^ 1)
        sibling = swapped(current, "leaf", level)
        locals_list.append(
            jnp.dot(sibling, tree_couple[own_node], preferred_element_type=jnp.float32)
        )
        lifted = jnp.dot(current, tree_up[own_node], preferred_element_type=jnp.float32) + jnp.dot(
            sibling, tree_up[other_node], preferred_element_type=jnp.float32
        )
        current = lifted.astype(jnp.bfloat16)
    downward = jnp.zeros(box_moment.shape, jnp.bfloat16)
    for level in reversed(range(levels)):
        level_first = 2 * device_total - 2 * (device_total >> level)
        own_node = level_first + (position >> level)
        carried = jnp.einsum(
            "rj,kj->rk", downward, tree_up[own_node], preferred_element_type=jnp.float32
        )
        downward = (locals_list[level] + carried).astype(jnp.bfloat16)
    leaf_down = jnp.einsum(
        "rj,ikj->irk", downward, leaf_transfer, preferred_element_type=jnp.float32
    )
    local_total = (far_term + leaf_down).astype(jnp.bfloat16)
    spread = jnp.einsum("irk,ikp->irp", local_total, leaf_basis, preferred_element_type=jnp.float32)
    return live_mask * (near + spread)


def column_sums(first_field, second_field):
    return jnp.sum(first_field * second_field, axis=(0, 2))


def global_norm(field):
    return jnp.sqrt(lax.psum(column_sums(field, field), "leaf") + epsilon)


def inner_sums(stacked):
    return lax.psum(stacked, "leaf")


def on_device(
    right_hand,
    leaf_live,
    near_index,
    near_tile,
    far_index,
    far_couple,
    leaf_basis,
    leaf_transfer,
    tree_up,
    tree_couple,
):

    def operator(vector):
        return apply_operator(
            vector,
            leaf_live,
            near_index,
            near_tile,
            far_index,
            far_couple,
            leaf_basis,
            leaf_transfer,
            tree_up,
            tree_couple,
        )

    live_mask = leaf_live.astype(jnp.float32)[:, None, None]
    start_vec = right_hand * live_mask
    norm_start = global_norm(start_vec)
    basis_one = start_vec / norm_start[None, :, None]
    image_one = operator(basis_one)
    first_inner = inner_sums(column_sums(basis_one, image_one)[None])[0]
    residue_one = image_one - first_inner[None, :, None] * basis_one
    first_length = global_norm(residue_one)
    basis_two = residue_one / first_length[None, :, None]
    image_two = operator(basis_two)
    both_inner = inner_sums(
        jnp.stack([column_sums(basis_one, image_two), column_sums(basis_two, image_two)])
    )
    cross_inner = both_inner[0]
    self_inner = both_inner[1]
    residue_two = (
        image_two - cross_inner[None, :, None] * basis_one - self_inner[None, :, None] * basis_two
    )
    second_length = global_norm(residue_two)
    basis_next = residue_two / second_length[None, :, None]
    hessenberg = jnp.stack(
        [norm_start, first_inner, first_length, cross_inner, self_inner, second_length]
    )
    return (basis_next, hessenberg)


def solution(mesh):
    placed = (
        P("leaf", None, None),
        P("leaf"),
        P("leaf", None),
        P("leaf", None, None, None),
        P("leaf", None),
        P("leaf", None, None, None),
        P("leaf", None, None),
        P("leaf", None, None),
        P(),
        P(),
    )
    return jax.shard_map(
        on_device,
        mesh=mesh,
        in_specs=placed,
        out_specs=(P("leaf", None, None), P()),
        check_vma=False,
    )
```

profile of v0, /device:TPU:1, one launch (start us, length us, event | category | flops | bytes accessed | tf_op | source)
XLA Modules:
  0.0 563.7 jit_solution(7283835769958912221)
XLA Ops:
  2.7 68.7 %psum.35 = f32[32]{0:T(128)S(1)} all-reduce(f32[32]{0:T(128)S(1)} %multiply_reduce_fusion.5), channel_id=1, replica_groups=mesh['leaf'=128] {'leaf'}, use_global_device_ids=true, to_apply=%region_1.0 | all-reduce | flops 32 | bytes 256 | tf_op jit(solution)/shard_map/psum | solution.py:94
  72.0 1.9 multiply_convert_fusion.1
  73.8 1.4 convolution_convert_fusion.1
  75.2 2.6 collective-permute-start.2
  77.8 2.4 collective-permute-start.3
  80.2 3.2 collective-permute-start
  83.4 1.9 collective-permute-start.1
  86.2 12.0 %constant_dynamic-slice_fusion.2 = (bf16[1,64,64]{0,2,1:T(8,128)(2,1)}, bf16[1,64,64]{0,2,1:T(8,128)(2,1)}, bf16[1,64,64]{0,2,1:T(8,128)(2,1)}, bf16[1,64,64]{0,...) fusion(bf16[254,64,64]{0,2,1:T(8,128)(2,1)} %param.18, ...), kind=kLoop, calls=%fused_computation.177 | loop fusion | bytes 213044 | tf_op jit(solution)/shard_map/dynamic_slice | solution.py:70
  98.2 1.7 copy.41
  99.8 1.4 fusion.124
  102.3 1.4 fusion.52
  103.8 9.0 %constant_dynamic-slice_fusion.19 = (bf16[1,64,64]{0,2,1:T(8,128)(2,1)S(1)}, bf16[1,64,64]{0,2,1:T(8,128)(2,1)}, bf16[1,64,64]{0,2,1:T(8,128)(2,1)}, bf16[1,64,6...) fusion(bf16[254,64,64]{0,2,1:T(8,128)(2,1)} %param.19, ...), kind=kLoop, calls=%fused_computation.194 | loop fusion | bytes 114716 | tf_op jit(solution)/shard_map/dynamic_slice | solution.py:67
  119.2 2.3 copy.42
  121.5 2.3 copy.44
  123.8 2.3 copy.45
  126.0 2.3 copy.47
  128.3 2.3 copy.48
  130.6 2.3 copy.50
  132.8 2.3 copy.51
  135.1 2.3 copy.53
  137.4 2.3 copy.54
  139.7 2.3 copy.56
  141.9 2.3 copy.57
  145.6 1.4 reshape.13
  147.8 1.8 collective-permute-start.5
  151.5 3.3 collective-permute-start.6
  156.7 4.8 collective-permute-start.7
  163.4 3.6 collective-permute-start.8
  168.9 5.7 %collective-permute-start.9 = (bf16[32,64]{1,0:T(8,128)(2,1)S(1)}, bf16[32,64]{1,0:T(8,128)(2,1)S(1)}, u32[]{:S(2)}, u32[]{:S(2)}) collective-permute-start(bf16[32,64]{1,0:T(8,128)(2,1)S(1)} %fusion.21), channel_id=1, source_target_pairs={{0,32},{1,33},{2,34},{3,35},{4,36},{5,37},{6,38},{7,39},{8,40},{9,... | collective-permute-start | bytes 12296 | tf_op jit(solution)/shard_map/ppermute | solution.py:23
  175.6 1.4 fusion.23
  177.0 3.1 collective-permute-start.10
  181.4 2.3 copy.58
  183.6 2.3 copy.55
  185.9 2.3 copy.52
  188.2 2.3 copy.49
  190.4 2.3 copy.46
  192.7 2.3 copy.43
  203.9 1.8 gather_fusion.1
  205.7 1.7 convolution_bitcast_fusion.5
  208.8 2.1 pad_maximum_fusion
  211.0 3.0 gather_fusion
  214.0 8.1 %multiply_reduce_fusion.4 = (f32[32]{0:T(128)S(1)}, f32[16,32,256]{2,1,0:T(8,128)}) fusion(f32[32]{0:T(128)S(1)} %copy-done.19, f32[16,32,256]{2,1,0:T(8,128)S(1)} %copy-done.1, f32[16]{0:T(128)S(1)} %copy-done.11, f32[16,32,256]{2,1,0:T(8,128)} %fusion.9, bf16[16,6,32,256]{3,2,1,0:T(8,128)(2,1)} %bitcast.261, bf16[16,6,256,256]{3,2,1,0:T(8,128)(2,1)} %param.13), kind=kOutput, calls=%fused_computation.101 | convolution fusion | flops 403439584 | bytes 15728960 | tf_op jit(solution)/shard_map/inrp,inpq->irq/dot_general | solution.py:46
  222.2 67.2 %psum.36 = f32[1,32]{1,0:T(1,128)S(1)} all-reduce(f32[1,32]{1,0:T(1,128)S(1)} %bitcast.268), channel_id=1, replica_groups=mesh['leaf'=128] {'leaf'}, use_global_device_ids=true, to_apply=%region_3.0 | all-reduce | flops 32 | bytes 256 | tf_op jit(solution)/shard_map/psum | solution.py:98
  290.7 62.8 %psum.37 = f32[32]{0:T(128)S(1)} all-reduce(f32[32]{0:T(128)S(1)} %multiply_reduce_fusion.3), channel_id=1, replica_groups=mesh['leaf'=128] {'leaf'}, use_global_device_ids=true, to_apply=%region_5.0 | all-reduce | flops 32 | bytes 256 | tf_op jit(solution)/shard_map/psum | solution.py:94
  354.1 2.2 multiply_convert_fusion
  363.5 1.7 collective-permute-start.17
  366.0 1.4 collective-permute-done.17
  371.6 1.7 collective-permute-start.19
  374.2 1.5 collective-permute-done.19
  377.9 1.4 collective-permute-done.20
  380.2 1.7 collective-permute-start.21
  381.9 8.1 %collective-permute-start.11 = (bf16[16,32,256]{2,1,0:T(8,128)(2,1)}, bf16[16,32,256]{2,1,0:T(8,128)(2,1)}, u32[]{:S(2)}, u32[]{:S(2)}) collective-permute-start(bf16[16,32,256]{2,1,0:T(8,128)(2,1)} %get-tuple-element.6), channel_id=1, source_target_pairs={{0,1},{1,2},{2,3},{3,4},{4,5},{5,6},{6,7},{7,8},{8,9},{9,10},{10,1... | collective-permute-start | bytes 786440 | tf_op jit(solution)/shard_map/ppermute | solution.py:16
  390.0 1.9 collective-permute-start.12
  391.9 3.6 collective-permute-start.13
  395.5 2.1 collective-permute-start.14
  406.2 1.8 gather_fusion.3
  408.0 2.4 convolution_bitcast_fusion.3
  410.4 2.2 fusion.8
  413.9 1.9 gather_fusion.2
  415.8 8.4 %multiply_reduce_fusion.2 = (f32[32]{0:T(128)S(1)}, f32[32]{0:T(128)S(1)}, f32[16,32,256]{2,1,0:T(8,128)}) fusion(f32[32]{0:T(128)S(1)} %copy-done.20, f32[16,32,256]{2,1,0:T(8,128)S(1)} %copy-done.1, f32[16]{0:T(128)S(1)} %copy-done.12, f32[16,32,256]{2,1,0:T(8,128)} %get-tuple-element.7, f32[16,32,256]{2,1,0:T(8,128)} %fusion.8, ...), kind=kOutput, calls=%fused_computation.97 | convolution fusion | flops 403701696 | bytes 16253376 | tf_op jit(solution)/shard_map/inrp,inpq->irq/dot_general | solution.py:46
  424.2 70.6 %psum.38 = f32[2,32]{1,0:T(2,128)S(1)} all-reduce(f32[2,32]{1,0:T(2,128)S(1)} %pad_maximum_fusion.4), channel_id=1, replica_groups=mesh['leaf'=128] {'leaf'}, use_global_device_ids=true, to_apply=%region_8.0 | all-reduce | flops 64 | bytes 512 | tf_op jit(solution)/shard_map/psum | solution.py:98
  494.9 2.1 multiply_reduce_fusion
  497.0 64.1 %psum.39 = f32[32]{0:T(128)S(1)} all-reduce(f32[32]{0:T(128)S(1)} %get-tuple-element.4), channel_id=1, replica_groups=mesh['leaf'=128] {'leaf'}, use_global_device_ids=true, to_apply=%region_10.0 | all-reduce | flops 32 | bytes 256 | tf_op jit(solution)/shard_map/psum | solution.py:94
  561.1 2.0 broadcast_divide_fusion
  (135 shorter events, 61.5 us)
Async XLA Ops:
  0.6 205.1 %copy-start = (bf16[16,8,64,64]{3,2,1,0:T(8,128)(2,1)S(1)}, bf16[16,8,64,64]{3,2,1,0:T(8,128)(2,1)}, u32[]{:S(2)}) copy-start(bf16[16,8,64,64]{3,2,1,0:T(8,128)(2,1)} %param.15) | copy-start | bytes 3145732
  0.6 84.7 %copy-start.4 = (bf16[16,64,64]{2,1,0:T(8,128)(2,1)S(1)}, bf16[16,64,64]{2,1,0:T(8,128)(2,1)}, u32[]{:S(2)}) copy-start(bf16[16,64,64]{2,1,0:T(8,128)(2,1)} %param.17) | copy-start | bytes 393220
  1.5 84.7 %copy-start.10 = (f32[16]{0:T(128)}, f32[16]{0:T(128)S(1)}, u32[]{:S(2)}) copy-start(f32[16]{0:T(128)S(1)} %convert_element_type.107) | copy-start | bytes 196
  72.0 14.2 %copy-start.18 = (f32[32]{0:T(128)}, f32[32]{0:T(128)S(1)}, u32[]{:S(2)}) copy-start(f32[32]{0:T(128)S(1)} %get-tuple-element.35) | copy-start | bytes 388
  75.2 127.6 %collective-permute-start.2 = (bf16[16,32,64]{2,1,0:T(8,128)(2,1)S(1)}, bf16[16,32,64]{2,1,0:T(8,128)(2,1)}, u32[]{:S(2)}, u32[]{:S(2)}) collective-permute-start(bf16[16,32,64]{2,1,0:T(8,128)(2,1)S(1)} %convolution_convert_fusion.1), channel_id=1, source_target_pairs={{0,1},{1,2},{2,3},{3,4},{4,5},{5,6},{6,7},{7,8},{8,9},{9,10},{10,1... | collective-permute-start | bytes 196616 | tf_op jit(solution)/shard_map/ppermute | solution.py:16
  77.8 125.0 %collective-permute-start.3 = (bf16[16,32,64]{2,1,0:T(8,128)(2,1)S(1)}, bf16[16,32,64]{2,1,0:T(8,128)(2,1)}, u32[]{:S(2)}, u32[]{:S(2)}) collective-permute-start(bf16[16,32,64]{2,1,0:T(8,128)(2,1)S(1)} %convolution_convert_fusion.1), channel_id=1, source_target_pairs={{1,0},{2,1},{3,2},{4,3},{5,4},{6,5},{7,6},{8,7},{9,8},{10,9},{11,1... | collective-permute-start | bytes 196616 | tf_op jit(solution)/shard_map/ppermute | solution.py:17
  80.2 128.6 %collective-permute-start = (bf16[16,32,256]{2,1,0:T(8,128)(2,1)}, bf16[16,32,256]{2,1,0:T(8,128)(2,1)}, u32[]{:S(2)}, u32[]{:S(2)}) collective-permute-start(bf16[16,32,256]{2,1,0:T(8,128)(2,1)} %multiply_convert_fusion.1), channel_id=1, source_target_pairs={{0,1},{1,2},{2,3},{3,4},{4,5},{5,6},{6,7},{7,8},{8,9},{9,10},{10,1... | collective-permute-start | bytes 786440 | tf_op jit(solution)/shard_map/ppermute | solution.py:16
  83.4 125.4 %collective-permute-start.1 = (bf16[16,32,256]{2,1,0:T(8,128)(2,1)}, bf16[16,32,256]{2,1,0:T(8,128)(2,1)}, u32[]{:S(2)}, u32[]{:S(2)}) collective-permute-start(bf16[16,32,256]{2,1,0:T(8,128)(2,1)} %multiply_convert_fusion.1), channel_id=1, source_target_pairs={{1,0},{2,1},{3,2},{4,3},{5,4},{6,5},{7,6},{8,7},{9,8},{10,9},{11,1... | collective-permute-start | bytes 786440 | tf_op jit(solution)/shard_map/ppermute | solution.py:17
  86.2 60.8 %collective-permute-start.4 = (bf16[32,64]{1,0:T(8,128)(2,1)}, bf16[32,64]{1,0:T(8,128)(2,1)}, u32[]{:S(2)}, u32[]{:S(2)}) collective-permute-start(bf16[32,64]{1,0:T(8,128)(2,1)} %fusion.10), channel_id=1, source_target_pairs={{0,1},{1,0},{2,3},{3,2},{4,5},{5,4},{6,7},{7,6},{8,9},{9,8},{10,11... | collective-permute-start | bytes 12296 | tf_op jit(solution)/shard_map/ppermute | solution.py:23
  147.8 2.9 collective-permute-start.5
  150.7 26.4 %copy-start.13 = (bf16[32,64]{1,0:T(8,128)(2,1)}, bf16[32,64]{1,0:T(8,128)(2,1)S(1)}, u32[]{:S(2)}) copy-start(bf16[32,64]{1,0:T(8,128)(2,1)S(1)} %collective-permute-done.5) | copy-start | bytes 12292
  151.5 4.4 collective-permute-start.6
  155.9 24.2 %copy-start.14 = (bf16[32,64]{1,0:T(8,128)(2,1)}, bf16[32,64]{1,0:T(8,128)(2,1)S(1)}, u32[]{:S(2)}) copy-start(bf16[32,64]{1,0:T(8,128)(2,1)S(1)} %collective-permute-done.6) | copy-start | bytes 12292
  156.7 5.8 %collective-permute-start.7 = (bf16[32,64]{1,0:T(8,128)(2,1)S(1)}, bf16[32,64]{1,0:T(8,128)(2,1)S(1)}, u32[]{:S(2)}, u32[]{:S(2)}) collective-permute-start(bf16[32,64]{1,0:T(8,128)(2,1)S(1)} %fusion.17), channel_id=1, source_target_pairs={{0,8},{1,9},{2,10},{3,11},{4,12},{5,13},{6,14},{7,15},{8,0},{9,1},... | collective-permute-start | bytes 12296 | tf_op jit(solution)/shard_map/ppermute | solution.py:23
  162.5 18.8 %copy-start.15 = (bf16[32,64]{1,0:T(8,128)(2,1)}, bf16[32,64]{1,0:T(8,128)(2,1)S(1)}, u32[]{:S(2)}) copy-start(bf16[32,64]{1,0:T(8,128)(2,1)S(1)} %collective-permute-done.7) | copy-start | bytes 12292
  163.4 4.6 collective-permute-start.8
  168.0 13.4 %copy-start.16 = (bf16[32,64]{1,0:T(8,128)(2,1)}, bf16[32,64]{1,0:T(8,128)(2,1)S(1)}, u32[]{:S(2)}) copy-start(bf16[32,64]{1,0:T(8,128)(2,1)S(1)} %collective-permute-done.8) | copy-start | bytes 12292
  168.9 6.7 %collective-permute-start.9 = (bf16[32,64]{1,0:T(8,128)(2,1)S(1)}, bf16[32,64]{1,0:T(8,128)(2,1)S(1)}, u32[]{:S(2)}, u32[]{:S(2)}) collective-permute-start(bf16[32,64]{1,0:T(8,128)(2,1)S(1)} %fusion.21), channel_id=1, source_target_pairs={{0,32},{1,33},{2,34},{3,35},{4,36},{5,37},{6,38},{7,39},{8,40},{9,... | collective-permute-start | bytes 12296 | tf_op jit(solution)/shard_map/ppermute | solution.py:23
  175.6 5.8 %copy-start.17 = (bf16[32,64]{1,0:T(8,128)(2,1)}, bf16[32,64]{1,0:T(8,128)(2,1)S(1)}, u32[]{:S(2)}) copy-start(bf16[32,64]{1,0:T(8,128)(2,1)S(1)} %collective-permute-done.9) | copy-start | bytes 12292
  177.0 19.0 %collective-permute-start.10 = (bf16[32,64]{1,0:T(8,128)(2,1)}, bf16[32,64]{1,0:T(8,128)(2,1)}, u32[]{:S(2)}, u32[]{:S(2)}) collective-permute-start(bf16[32,64]{1,0:T(8,128)(2,1)} %fusion.23), channel_id=1, source_target_pairs={{0,64},{1,65},{2,66},{3,67},{4,68},{5,69},{6,70},{7,71},{8,72},{9,... | collective-permute-start | bytes 12296 | tf_op jit(solution)/shard_map/ppermute | solution.py:23
  205.7 1.8 copy-start.2
  207.5 3.5 copy-start.8
  208.8 5.2 copy-start.1
  208.8 5.2 copy-start.11
  208.8 5.2 copy-start.19
  289.4 66.9 %copy-start.21 = (f32[1,32]{1,0:T(1,128)}, f32[1,32]{1,0:T(1,128)S(1)}, u32[]{:S(2)}) copy-start(f32[1,32]{1,0:T(1,128)S(1)} %psum.36) | copy-start | bytes 388
  357.5 46.9 %copy-start.6 = (bf16[16,32,64]{2,1,0:T(8,128)(2,1)}, bf16[16,32,64]{2,1,0:T(8,128)(2,1)S(1)}, u32[]{:S(2)}) copy-start(bf16[16,32,64]{2,1,0:T(8,128)(2,1)S(1)} %convolution_convert_fusion) | copy-start | bytes 196612
  357.7 1.5 collective-permute-start.15
  360.1 2.5 collective-permute-start.16
  363.5 4.0 collective-permute-start.17
  368.3 2.5 collective-permute-start.18
  371.6 4.1 collective-permute-start.19
  376.6 2.8 collective-permute-start.20
  380.2 17.5 %collective-permute-start.21 = (bf16[32,64]{1,0:T(8,128)(2,1)S(1)}, bf16[32,64]{1,0:T(8,128)(2,1)S(1)}, u32[]{:S(2)}, u32[]{:S(2)}) collective-permute-start(bf16[32,64]{1,0:T(8,128)(2,1)S(1)} %fusion.36), channel_id=1, source_target_pairs={{0,64},{1,65},{2,66},{3,67},{4,68},{5,69},{6,70},{7,71},{8,72},{9,... | collective-permute-start | bytes 12296 | tf_op jit(solution)/shard_map/ppermute | solution.py:23
  381.9 30.8 %collective-permute-start.11 = (bf16[16,32,256]{2,1,0:T(8,128)(2,1)}, bf16[16,32,256]{2,1,0:T(8,128)(2,1)}, u32[]{:S(2)}, u32[]{:S(2)}) collective-permute-start(bf16[16,32,256]{2,1,0:T(8,128)(2,1)} %get-tuple-element.6), channel_id=1, source_target_pairs={{0,1},{1,2},{2,3},{3,4},{4,5},{5,6},{6,7},{7,8},{8,9},{9,10},{10,1... | collective-permute-start | bytes 786440 | tf_op jit(solution)/shard_map/ppermute | solution.py:16
  390.0 22.7 %collective-permute-start.12 = (bf16[16,32,256]{2,1,0:T(8,128)(2,1)}, bf16[16,32,256]{2,1,0:T(8,128)(2,1)}, u32[]{:S(2)}, u32[]{:S(2)}) collective-permute-start(bf16[16,32,256]{2,1,0:T(8,128)(2,1)} %get-tuple-element.6), channel_id=1, source_target_pairs={{1,0},{2,1},{3,2},{4,3},{5,4},{6,5},{7,6},{8,7},{9,8},{10,9},{11,1... | collective-permute-start | bytes 786440 | tf_op jit(solution)/shard_map/ppermute | solution.py:17
  391.9 12.5 %collective-permute-start.13 = (bf16[16,32,64]{2,1,0:T(8,128)(2,1)S(1)}, bf16[16,32,64]{2,1,0:T(8,128)(2,1)S(1)}, u32[]{:S(2)}, u32[]{:S(2)}) collective-permute-start(bf16[16,32,64]{2,1,0:T(8,128)(2,1)S(1)} %convolution_convert_fusion), channel_id=1, source_target_pairs={{0,1},{1,2},{2,3},{3,4},{4,5},{5,6},{6,7},{7,8},{8,9},{9,10},{10,1... | collective-permute-start | bytes 196616 | tf_op jit(solution)/shard_map/ppermute | solution.py:16
  395.5 9.5 %collective-permute-start.14 = (bf16[16,32,64]{2,1,0:T(8,128)(2,1)S(1)}, bf16[16,32,64]{2,1,0:T(8,128)(2,1)}, u32[]{:S(2)}, u32[]{:S(2)}) collective-permute-start(bf16[16,32,64]{2,1,0:T(8,128)(2,1)S(1)} %convolution_convert_fusion), channel_id=1, source_target_pairs={{1,0},{2,1},{3,2},{4,3},{5,4},{6,5},{7,6},{8,7},{9,8},{10,9},{11,1... | collective-permute-start | bytes 196616 | tf_op jit(solution)/shard_map/ppermute | solution.py:17
  404.4 0.7 copy-start.7
  408.0 2.4 copy-start.5
  410.4 3.5 copy-start.9
  412.7 3.1 copy-start.12
  412.7 3.1 copy-start.20
  415.8 79.0 %copy-start.3 = (f32[16,32,256]{2,1,0:T(8,128)S(1)}, f32[16,32,256]{2,1,0:T(8,128)}, u32[]{:S(2)}) copy-start(f32[16,32,256]{2,1,0:T(8,128)} %get-tuple-element.7) | copy-start | bytes 1572868
  424.2 138.9 %copy-start.22 = (f32[1,32]{1,0:T(1,128)S(1)}, f32[1,32]{1,0:T(1,128)}, u32[]{:S(2)}) copy-start(f32[1,32]{1,0:T(1,128)} %copy-done.21) | copy-start | bytes 388
  424.2 138.9 %copy-start.23 = (f32[1,32]{1,0:T(1,128)S(1)}, f32[1,32]{1,0:T(1,128)}, u32[]{:S(2)}) copy-start(f32[1,32]{1,0:T(1,128)} %get-tuple-element.34) | copy-start | bytes 388
  424.2 138.9 %copy-start.24 = (f32[1,32]{1,0:T(1,128)S(1)}, f32[1,32]{1,0:T(1,128)}, u32[]{:S(2)}) copy-start(f32[1,32]{1,0:T(1,128)} %get-tuple-element.32) | copy-start | bytes 388
where the time goes:
time: 570 us; the launch traced here: 564 us
  blocking collectives  333 us (58%)
  local copies, waits for them, and re-layouts  78.7 us (14%)
  matrix products  63.4 us (11%)
  starting transfers between devices  56.1 us (10%)
  other arithmetic  23.2 us (4%)
  waiting for transfers between devices  7.84 us (1%)
    psum x3, blocking collectives, global_norm(): return jnp.sqrt(lax.psum(column_sums(field, field), 'leaf') + epsilon)  196 us
    psum x2, blocking collectives, inner_sums(): return lax.psum(stacked, 'leaf')  138 us
    unnamed x70, local copies, waits for them, and re-layouts  43.1 us
    ppermute x14, starting transfers between devices, swapped(): lax.ppermute(array, axis, [(i, i ^ 1 << stride) for i in range(lax.axis_s...  30.2 us
    ppermute x4, starting transfers between devices, with_halo(): before = lax.ppermute(last, axis, up)  17.5 us
    dot_general x2, matrix products, apply_operator(): jnp.einsum('inrp,inpq->irq', columns, near_tile, preferred_element_type=j...  16.5 us
    dot_general x13, matrix products, apply_operator(): jnp.einsum('rj,kj->rk', downward, tree_up[own_node], preferred_element_ty...  13.2 us
    dynamic_slice x1, local copies, waits for them, and re-layouts, apply_operator(): tree_up[other_node]  12 us
  transfers between devices with their start and end apart: 22, of which 11 were waited for; matrix products, arithmetic and copies ran while one was open for 21% of the time, Pallas kernels for 0%

commit v1 on v0

--- a/solution.py
+++ b/solution.py
@@ -4,6 +4,11 @@
 from jax.sharding import PartitionSpec as P
 
 epsilon = 1e-06
+
+
+def gather_and_add(shard, axis):
+    parts = lax.all_gather(shard, axis)
+    return jnp.sum(parts, axis=0)
 
 
 def with_halo(array, sides, width):
@@ -91,7 +96,7 @@
 
 
 def global_norm(field):
-    return jnp.sqrt(lax.psum(column_sums(field, field), "leaf") + epsilon)
+    return jnp.sqrt(gather_and_add(column_sums(field, field), "leaf") + epsilon)
 
 
 def inner_sums(stacked):

time: 570 us -> 571 us (level)
    unnamed x0 -> x3, blocking collectives: none -> 196 us
    psum x3 -> x0, blocking collectives: 196 us -> none  [global_norm(): return jnp.sqrt(lax.psum(column_sums(field, field), 'leaf') + epsilon)]
    unnamed x70 -> x76, local copies, waits for them, and re-layouts: 43.1 us -> 44 us
where the time goes in v1:
time: 571 us; the launch traced here: 565 us
  blocking collectives  334 us (58%)
  local copies, waits for them, and re-layouts  79.8 us (14%)
  matrix products  63.4 us (11%)
  starting transfers between devices  56 us (10%)
  other arithmetic  23.4 us (4%)
  waiting for transfers between devices  7.88 us (1%)
    unnamed x3, blocking collectives  196 us
    psum x2, blocking collectives, inner_sums(): return lax.psum(stacked, 'leaf')  138 us
    unnamed x76, local copies, waits for them, and re-layouts  44 us
    ppermute x14, starting transfers between devices, swapped(): lax.ppermute(array, axis, [(i, i ^ 1 << stride) for i in range(lax.axis_s...  30.2 us
    ppermute x4, starting transfers between devices, with_halo(): before = lax.ppermute(last, axis, up)  17.4 us
    dot_general x2, matrix products, apply_operator(): jnp.einsum('inrp,inpq->irq', columns, near_tile, preferred_element_type=j...  16.5 us
    dot_general x13, matrix products, apply_operator(): jnp.einsum('rj,kj->rk', downward, tree_up[own_node], preferred_element_ty...  13.2 us
    dynamic_slice x1, local copies, waits for them, and re-layouts, apply_operator(): tree_up[other_node]  12 us
  transfers between devices with their start and end apart: 22, of which 11 were waited for; matrix products, arithmetic and copies ran while one was open for 21% of the time, Pallas kernels for 0%

profile of v1, /device:TPU:1, one launch (start us, length us, event | category | flops | bytes accessed | tf_op | source)
XLA Modules:
  0.0 565.2 jit_solution(12844319850355305371)
XLA Ops:
  3.0 68.7 %all-reduce = f32[4096]{0:T(1024)S(1)} all-reduce(f32[4096]{0:T(1024)S(1)} %dynamic-update-slice), channel_id=2, replica_groups=mesh['leaf'=128] {'leaf'}, use_global_device_ids=true, to_apply=%add | all-reduce | flops 4096 | bytes 32768
  72.4 1.9 multiply_convert_fusion.1
  74.3 1.4 convolution_convert_fusion.1
  75.7 2.6 collective-permute-start.2
  78.3 2.4 collective-permute-start.3
  80.7 3.2 collective-permute-start
  83.9 1.9 collective-permute-start.1
  86.6 12.0 %constant_dynamic-slice_fusion.2 = (bf16[1,64,64]{0,2,1:T(8,128)(2,1)}, bf16[1,64,64]{0,2,1:T(8,128)(2,1)}, bf16[1,64,64]{0,2,1:T(8,128)(2,1)}, bf16[1,64,64]{0,...) fusion(bf16[254,64,64]{0,2,1:T(8,128)(2,1)} %param.18, ...), kind=kLoop, calls=%fused_computation.177 | loop fusion | bytes 213044 | tf_op jit(solution)/shard_map/dynamic_slice | solution.py:75
  98.6 1.7 copy.41
  100.3 1.4 fusion.124
  102.8 1.4 fusion.52
  104.2 9.0 %constant_dynamic-slice_fusion.19 = (bf16[1,64,64]{0,2,1:T(8,128)(2,1)S(1)}, bf16[1,64,64]{0,2,1:T(8,128)(2,1)}, bf16[1,64,64]{0,2,1:T(8,128)(2,1)}, bf16[1,64,6...) fusion(bf16[254,64,64]{0,2,1:T(8,128)(2,1)} %param.19, ...), kind=kLoop, calls=%fused_computation.194 | loop fusion | bytes 114716 | tf_op jit(solution)/shard_map/dynamic_slice | solution.py:72
  119.6 2.3 copy.42
  121.9 2.3 copy.44
  124.1 2.3 copy.45
  126.4 2.3 copy.47
  128.7 2.3 copy.48
  131.0 2.3 copy.50
  133.2 2.3 copy.51
  135.5 2.3 copy.53
  137.8 2.3 copy.54
  140.1 2.3 copy.56
  142.3 2.3 copy.57
  145.9 1.4 reshape.61
  148.2 1.8 collective-permute-start.5
  151.9 3.4 collective-permute-start.6
  157.1 4.8 collective-permute-start.7
  163.8 3.7 collective-permute-start.8
  169.4 5.7 %collective-permute-start.9 = (bf16[32,64]{1,0:T(8,128)(2,1)S(1)}, bf16[32,64]{1,0:T(8,128)(2,1)S(1)}, u32[]{:S(2)}, u32[]{:S(2)}) collective-permute-start(bf16[32,64]{1,0:T(8,128)(2,1)S(1)} %fusion.21), channel_id=1, source_target_pairs={{0,32},{1,33},{2,34},{3,35},{4,36},{5,37},{6,38},{7,39},{8,40},{9,... | collective-permute-start | bytes 12296 | tf_op jit(solution)/shard_map/ppermute | solution.py:28
  176.1 1.4 fusion.23
  177.5 3.0 collective-permute-start.10
  181.8 2.3 copy.58
  184.1 2.3 copy.55
  186.4 2.3 copy.52
  188.6 2.3 copy.49
  190.9 2.3 copy.46
  193.2 2.3 copy.43
  204.4 1.8 gather_fusion.1
  206.2 1.7 convolution_bitcast_fusion.5
  209.3 2.1 pad_maximum_fusion
  211.4 3.1 gather_fusion
  214.5 8.1 %multiply_reduce_fusion.4 = (f32[32]{0:T(128)S(1)}, f32[16,32,256]{2,1,0:T(8,128)}) fusion(f32[32]{0:T(128)S(1)} %copy-done.19, f32[16,32,256]{2,1,0:T(8,128)S(1)} %copy-done.1, f32[16]{0:T(128)S(1)} %copy-done.11, f32[16,32,256]{2,1,0:T(8,128)} %fusion.9, bf16[16,6,32,256]{3,2,1,0:T(8,128)(2,1)} %bitcast.261, bf16[16,6,256,256]{3,2,1,0:T(8,128)(2,1)} %param.13), kind=kOutput, calls=%fused_computation.101 | convolution fusion | flops 403439584 | bytes 15728960 | tf_op jit(solution)/shard_map/inrp,inpq->irq/dot_general | solution.py:51
  222.6 67.2 %psum.14 = f32[1,32]{1,0:T(1,128)S(1)} all-reduce(f32[1,32]{1,0:T(1,128)S(1)} %bitcast.268), channel_id=1, replica_groups=mesh['leaf'=128] {'leaf'}, use_global_device_ids=true, to_apply=%region_3.0 | all-reduce | flops 32 | bytes 256 | tf_op jit(solution)/shard_map/psum | solution.py:103
  291.5 63.0 %all-reduce.1 = f32[4096]{0:T(1024)S(1)} all-reduce(f32[4096]{0:T(1024)S(1)} %dynamic-update-slice.1), channel_id=3, replica_groups=mesh['leaf'=128] {'leaf'}, use_global_device_ids=true, to_apply=%add.1 | all-reduce | flops 4096 | bytes 32768
  355.1 2.2 multiply_convert_fusion
  364.5 1.7 collective-permute-start.17
  367.0 1.5 collective-permute-done.17
  372.7 1.7 collective-permute-start.19
  375.2 1.5 collective-permute-done.19
  378.9 1.5 collective-permute-done.20
  381.2 1.7 collective-permute-start.21
  382.9 8.1 %collective-permute-start.11 = (bf16[16,32,256]{2,1,0:T(8,128)(2,1)}, bf16[16,32,256]{2,1,0:T(8,128)(2,1)}, u32[]{:S(2)}, u32[]{:S(2)}) collective-permute-start(bf16[16,32,256]{2,1,0:T(8,128)(2,1)} %get-tuple-element.6), channel_id=1, source_target_pairs={{0,1},{1,2},{2,3},{3,4},{4,5},{5,6},{6,7},{7,8},{8,9},{9,10},{10,1... | collective-permute-start | bytes 786440 | tf_op jit(solution)/shard_map/ppermute | solution.py:21
  391.0 1.9 collective-permute-start.12
  392.9 3.6 collective-permute-start.13
  396.5 2.1 collective-permute-start.14
  407.2 1.8 gather_fusion.3
  409.0 2.4 convolution_bitcast_fusion.3
  411.4 2.2 fusion.8
  414.9 1.9 gather_fusion.2
  416.8 8.4 %multiply_reduce_fusion.2 = (f32[32]{0:T(128)S(1)}, f32[32]{0:T(128)S(1)}, f32[16,32,256]{2,1,0:T(8,128)}) fusion(f32[32]{0:T(128)S(1)} %copy-done.20, f32[16,32,256]{2,1,0:T(8,128)S(1)} %copy-done.1, f32[16]{0:T(128)S(1)} %copy-done.12, f32[16,32,256]{2,1,0:T(8,128)} %get-tuple-element.7, f32[16,32,256]{2,1,0:T(8,128)} %fusion.8, ...), kind=kOutput, calls=%fused_computation.97 | convolution fusion | flops 403701696 | bytes 16253376 | tf_op jit(solution)/shard_map/inrp,inpq->irq/dot_general | solution.py:51
  425.2 70.7 %psum.15 = f32[2,32]{1,0:T(2,128)S(1)} all-reduce(f32[2,32]{1,0:T(2,128)S(1)} %pad_maximum_fusion.4), channel_id=1, replica_groups=mesh['leaf'=128] {'leaf'}, use_global_device_ids=true, to_apply=%region_8.0 | all-reduce | flops 64 | bytes 512 | tf_op jit(solution)/shard_map/psum | solution.py:103
  495.9 2.1 multiply_reduce_fusion
  498.4 64.2 %all-reduce.2 = f32[4096]{0:T(1024)S(1)} all-reduce(f32[4096]{0:T(1024)S(1)} %dynamic-update-slice.2), channel_id=4, replica_groups=mesh['leaf'=128] {'leaf'}, use_global_device_ids=true, to_apply=%add.2 | all-reduce | flops 4096 | bytes 32768
  562.7 2.0 broadcast_divide_fusion
  (147 shorter events, 62.6 us)
Async XLA Ops:
  0.6 205.6 %copy-start = (bf16[16,8,64,64]{3,2,1,0:T(8,128)(2,1)S(1)}, bf16[16,8,64,64]{3,2,1,0:T(8,128)(2,1)}, u32[]{:S(2)}) copy-start(bf16[16,8,64,64]{3,2,1,0:T(8,128)(2,1)} %param.15) | copy-start | bytes 3145732
  0.6 85.1 %copy-start.4 = (bf16[16,64,64]{2,1,0:T(8,128)(2,1)S(1)}, bf16[16,64,64]{2,1,0:T(8,128)(2,1)}, u32[]{:S(2)}) copy-start(bf16[16,64,64]{2,1,0:T(8,128)(2,1)} %param.17) | copy-start | bytes 393220
  1.5 85.1 %copy-start.10 = (f32[16]{0:T(128)}, f32[16]{0:T(128)S(1)}, u32[]{:S(2)}) copy-start(f32[16]{0:T(128)S(1)} %convert_element_type.107) | copy-start | bytes 196
  72.4 14.2 %copy-start.18 = (f32[32]{0:T(128)}, f32[32]{0:T(128)S(1)}, u32[]{:S(2)}) copy-start(f32[32]{0:T(128)S(1)} %get-tuple-element.35) | copy-start | bytes 388
  75.7 127.6 %collective-permute-start.2 = (bf16[16,32,64]{2,1,0:T(8,128)(2,1)S(1)}, bf16[16,32,64]{2,1,0:T(8,128)(2,1)}, u32[]{:S(2)}, u32[]{:S(2)}) collective-permute-start(bf16[16,32,64]{2,1,0:T(8,128)(2,1)S(1)} %convolution_convert_fusion.1), channel_id=1, source_target_pairs={{0,1},{1,2},{2,3},{3,4},{4,5},{5,6},{6,7},{7,8},{8,9},{9,10},{10,1... | collective-permute-start | bytes 196616 | tf_op jit(solution)/shard_map/ppermute | solution.py:21
  78.3 125.1 %collective-permute-start.3 = (bf16[16,32,64]{2,1,0:T(8,128)(2,1)S(1)}, bf16[16,32,64]{2,1,0:T(8,128)(2,1)}, u32[]{:S(2)}, u32[]{:S(2)}) collective-permute-start(bf16[16,32,64]{2,1,0:T(8,128)(2,1)S(1)} %convolution_convert_fusion.1), channel_id=1, source_target_pairs={{1,0},{2,1},{3,2},{4,3},{5,4},{6,5},{7,6},{8,7},{9,8},{10,9},{11,1... | collective-permute-start | bytes 196616 | tf_op jit(solution)/shard_map/ppermute | solution.py:22
  80.7 128.6 %collective-permute-start = (bf16[16,32,256]{2,1,0:T(8,128)(2,1)}, bf16[16,32,256]{2,1,0:T(8,128)(2,1)}, u32[]{:S(2)}, u32[]{:S(2)}) collective-permute-start(bf16[16,32,256]{2,1,0:T(8,128)(2,1)} %multiply_convert_fusion.1), channel_id=1, source_target_pairs={{0,1},{1,2},{2,3},{3,4},{4,5},{5,6},{6,7},{7,8},{8,9},{9,10},{10,1... | collective-permute-start | bytes 786440 | tf_op jit(solution)/shard_map/ppermute | solution.py:21
  83.9 125.4 %collective-permute-start.1 = (bf16[16,32,256]{2,1,0:T(8,128)(2,1)}, bf16[16,32,256]{2,1,0:T(8,128)(2,1)}, u32[]{:S(2)}, u32[]{:S(2)}) collective-permute-start(bf16[16,32,256]{2,1,0:T(8,128)(2,1)} %multiply_convert_fusion.1), channel_id=1, source_target_pairs={{1,0},{2,1},{3,2},{4,3},{5,4},{6,5},{7,6},{8,7},{9,8},{10,9},{11,1... | collective-permute-start | bytes 786440 | tf_op jit(solution)/shard_map/ppermute | solution.py:22
  86.6 60.7 %collective-permute-start.4 = (bf16[32,64]{1,0:T(8,128)(2,1)}, bf16[32,64]{1,0:T(8,128)(2,1)}, u32[]{:S(2)}, u32[]{:S(2)}) collective-permute-start(bf16[32,64]{1,0:T(8,128)(2,1)} %fusion.10), channel_id=1, source_target_pairs={{0,1},{1,0},{2,3},{3,2},{4,5},{5,4},{6,7},{7,6},{8,9},{9,8},{10,11... | collective-permute-start | bytes 12296 | tf_op jit(solution)/shard_map/ppermute | solution.py:28
  148.2 2.8 collective-permute-start.5
  151.0 26.5 %copy-start.13 = (bf16[32,64]{1,0:T(8,128)(2,1)}, bf16[32,64]{1,0:T(8,128)(2,1)S(1)}, u32[]{:S(2)}) copy-start(bf16[32,64]{1,0:T(8,128)(2,1)S(1)} %collective-permute-done.5) | copy-start | bytes 12292
  151.9 4.4 collective-permute-start.6
  156.3 24.2 %copy-start.14 = (bf16[32,64]{1,0:T(8,128)(2,1)}, bf16[32,64]{1,0:T(8,128)(2,1)S(1)}, u32[]{:S(2)}) copy-start(bf16[32,64]{1,0:T(8,128)(2,1)S(1)} %collective-permute-done.6) | copy-start | bytes 12292
  157.1 5.8 %collective-permute-start.7 = (bf16[32,64]{1,0:T(8,128)(2,1)S(1)}, bf16[32,64]{1,0:T(8,128)(2,1)S(1)}, u32[]{:S(2)}, u32[]{:S(2)}) collective-permute-start(bf16[32,64]{1,0:T(8,128)(2,1)S(1)} %fusion.17), channel_id=1, source_target_pairs={{0,8},{1,9},{2,10},{3,11},{4,12},{5,13},{6,14},{7,15},{8,0},{9,1},... | collective-permute-start | bytes 12296 | tf_op jit(solution)/shard_map/ppermute | solution.py:28
  162.9 18.9 %copy-start.15 = (bf16[32,64]{1,0:T(8,128)(2,1)}, bf16[32,64]{1,0:T(8,128)(2,1)S(1)}, u32[]{:S(2)}) copy-start(bf16[32,64]{1,0:T(8,128)(2,1)S(1)} %collective-permute-done.7) | copy-start | bytes 12292
  163.8 4.8 collective-permute-start.8
  168.5 13.3 %copy-start.16 = (bf16[32,64]{1,0:T(8,128)(2,1)}, bf16[32,64]{1,0:T(8,128)(2,1)S(1)}, u32[]{:S(2)}) copy-start(bf16[32,64]{1,0:T(8,128)(2,1)S(1)} %collective-permute-done.8) | copy-start | bytes 12292
  169.4 6.7 %collective-permute-start.9 = (bf16[32,64]{1,0:T(8,128)(2,1)S(1)}, bf16[32,64]{1,0:T(8,128)(2,1)S(1)}, u32[]{:S(2)}, u32[]{:S(2)}) collective-permute-start(bf16[32,64]{1,0:T(8,128)(2,1)S(1)} %fusion.21), channel_id=1, source_target_pairs={{0,32},{1,33},{2,34},{3,35},{4,36},{5,37},{6,38},{7,39},{8,40},{9,... | collective-permute-start | bytes 12296 | tf_op jit(solution)/shard_map/ppermute | solution.py:28
  176.1 5.7 %copy-start.17 = (bf16[32,64]{1,0:T(8,128)(2,1)}, bf16[32,64]{1,0:T(8,128)(2,1)S(1)}, u32[]{:S(2)}) copy-start(bf16[32,64]{1,0:T(8,128)(2,1)S(1)} %collective-permute-done.9) | copy-start | bytes 12292
  177.5 19.0 %collective-permute-start.10 = (bf16[32,64]{1,0:T(8,128)(2,1)}, bf16[32,64]{1,0:T(8,128)(2,1)}, u32[]{:S(2)}, u32[]{:S(2)}) collective-permute-start(bf16[32,64]{1,0:T(8,128)(2,1)} %fusion.23), channel_id=1, source_target_pairs={{0,64},{1,65},{2,66},{3,67},{4,68},{5,69},{6,70},{7,71},{8,72},{9,... | collective-permute-start | bytes 12296 | tf_op jit(solution)/shard_map/ppermute | solution.py:28
  206.2 1.8 copy-start.2
  208.0 3.5 copy-start.8
  209.3 5.2 copy-start.1
  209.3 5.2 copy-start.11
  209.3 5.2 copy-start.19
  289.9 67.5 %copy-start.21 = (f32[1,32]{1,0:T(1,128)}, f32[1,32]{1,0:T(1,128)S(1)}, u32[]{:S(2)}) copy-start(f32[1,32]{1,0:T(1,128)S(1)} %psum.14) | copy-start | bytes 388
  358.5 46.9 %copy-start.6 = (bf16[16,32,64]{2,1,0:T(8,128)(2,1)}, bf16[16,32,64]{2,1,0:T(8,128)(2,1)S(1)}, u32[]{:S(2)}) copy-start(bf16[16,32,64]{2,1,0:T(8,128)(2,1)S(1)} %convolution_convert_fusion) | copy-start | bytes 196612
  358.8 1.5 collective-permute-start.15
  361.1 2.5 collective-permute-start.16
  364.5 4.0 collective-permute-start.17
  369.3 2.5 collective-permute-start.18
  372.7 4.1 collective-permute-start.19
  377.6 2.8 collective-permute-start.20
  381.2 17.5 %collective-permute-start.21 = (bf16[32,64]{1,0:T(8,128)(2,1)S(1)}, bf16[32,64]{1,0:T(8,128)(2,1)S(1)}, u32[]{:S(2)}, u32[]{:S(2)}) collective-permute-start(bf16[32,64]{1,0:T(8,128)(2,1)S(1)} %fusion.36), channel_id=1, source_target_pairs={{0,64},{1,65},{2,66},{3,67},{4,68},{5,69},{6,70},{7,71},{8,72},{9,... | collective-permute-start | bytes 12296 | tf_op jit(solution)/shard_map/ppermute | solution.py:28
  382.9 30.8 %collective-permute-start.11 = (bf16[16,32,256]{2,1,0:T(8,128)(2,1)}, bf16[16,32,256]{2,1,0:T(8,128)(2,1)}, u32[]{:S(2)}, u32[]{:S(2)}) collective-permute-start(bf16[16,32,256]{2,1,0:T(8,128)(2,1)} %get-tuple-element.6), channel_id=1, source_target_pairs={{0,1},{1,2},{2,3},{3,4},{4,5},{5,6},{6,7},{7,8},{8,9},{9,10},{10,1... | collective-permute-start | bytes 786440 | tf_op jit(solution)/shard_map/ppermute | solution.py:21
  391.0 22.7 %collective-permute-start.12 = (bf16[16,32,256]{2,1,0:T(8,128)(2,1)}, bf16[16,32,256]{2,1,0:T(8,128)(2,1)}, u32[]{:S(2)}, u32[]{:S(2)}) collective-permute-start(bf16[16,32,256]{2,1,0:T(8,128)(2,1)} %get-tuple-element.6), channel_id=1, source_target_pairs={{1,0},{2,1},{3,2},{4,3},{5,4},{6,5},{7,6},{8,7},{9,8},{10,9},{11,1... | collective-permute-start | bytes 786440 | tf_op jit(solution)/shard_map/ppermute | solution.py:22
  392.9 12.5 %collective-permute-start.13 = (bf16[16,32,64]{2,1,0:T(8,128)(2,1)S(1)}, bf16[16,32,64]{2,1,0:T(8,128)(2,1)S(1)}, u32[]{:S(2)}, u32[]{:S(2)}) collective-permute-start(bf16[16,32,64]{2,1,0:T(8,128)(2,1)S(1)} %convolution_convert_fusion), channel_id=1, source_target_pairs={{0,1},{1,2},{2,3},{3,4},{4,5},{5,6},{6,7},{7,8},{8,9},{9,10},{10,1... | collective-permute-start | bytes 196616 | tf_op jit(solution)/shard_map/ppermute | solution.py:21
  396.5 9.5 %collective-permute-start.14 = (bf16[16,32,64]{2,1,0:T(8,128)(2,1)S(1)}, bf16[16,32,64]{2,1,0:T(8,128)(2,1)}, u32[]{:S(2)}, u32[]{:S(2)}) collective-permute-start(bf16[16,32,64]{2,1,0:T(8,128)(2,1)S(1)} %convolution_convert_fusion), channel_id=1, source_target_pairs={{1,0},{2,1},{3,2},{4,3},{5,4},{6,5},{7,6},{8,7},{9,8},{10,9},{11,1... | collective-permute-start | bytes 196616 | tf_op jit(solution)/shard_map/ppermute | solution.py:22
  405.4 0.7 copy-start.7
  409.0 2.4 copy-start.5
  411.4 3.5 copy-start.9
  413.7 3.2 copy-start.12
  413.7 3.2 copy-start.20
  416.8 79.1 %copy-start.3 = (f32[16,32,256]{2,1,0:T(8,128)S(1)}, f32[16,32,256]{2,1,0:T(8,128)}, u32[]{:S(2)}) copy-start(f32[16,32,256]{2,1,0:T(8,128)} %get-tuple-element.7) | copy-start | bytes 1572868
  425.2 139.4 %copy-start.22 = (f32[1,32]{1,0:T(1,128)S(1)}, f32[1,32]{1,0:T(1,128)}, u32[]{:S(2)}) copy-start(f32[1,32]{1,0:T(1,128)} %copy-done.21) | copy-start | bytes 388
  425.2 139.4 %copy-start.23 = (f32[1,32]{1,0:T(1,128)S(1)}, f32[1,32]{1,0:T(1,128)}, u32[]{:S(2)}) copy-start(f32[1,32]{1,0:T(1,128)} %get-tuple-element.34) | copy-start | bytes 388
  425.2 139.4 %copy-start.24 = (f32[1,32]{1,0:T(1,128)S(1)}, f32[1,32]{1,0:T(1,128)}, u32[]{:S(2)}) copy-start(f32[1,32]{1,0:T(1,128)} %get-tuple-element.32) | copy-start | bytes 388
